TPU v7x, 128 devices: a whole 4x4x4 slice. The times are simulated.
128 devices in a mesh: probe: 4 (over z_hi, core), sx: 4 (over x), sy: 8 (over y, z_lo).
Axes of the slice: x: 4, y: 4, z: 4 (z_hi: 2, z_lo: 2; z = z_hi * 2 + z_lo), core: 2. Of those that a mesh axis runs over, the one named last changes fastest.
Arguments:
- probes: float32 [8, 128, 256, 256], P('probe', 'sx', 'sy'), may hold values from -6 to 6
- velocity: float32 [3, 128, 256, 256], P(None, 'sx', 'sy'), may hold values from -0.15 to 0.15
- diffusivity: float32 [128, 256, 256], P('sx', 'sy'), may hold values from 0.02 to 0.15
- obs_weight: float32 [128, 256, 256], P('sx', 'sy'), may hold values from 0.05 to 1
Outputs:
- basis_fields: float32 [8, 128, 256, 256], P('probe', 'sx', 'sy')
- projected_hessian: float32 [8, 8], replicated
All inputs are finite; a program needn't handle non-finite values.
Results may differ from a plain program's by a relative error of at most 0.00013.
Values sent between devices are 32-bit elements; how exact they have to be, the bound alone decides.
A program may use at most 128 MiB of HBM per device.

v0:
```python
import jax
import jax.numpy as jnp
from jax import lax
from jax.sharding import PartitionSpec as P

STEPS = 4


def extended(value, sides, width):
    for axis, dim in sides:
        devices, length = (lax.axis_size(axis), value.shape[dim])
        up = [(i, (i + 1) % devices) for i in range(devices - 1)]
        down = [(j, i) for i, j in up]
        last = lax.slice_in_dim(value, length - width, length, axis=dim)
        leading = lax.slice_in_dim(value, 0, width, axis=dim)
        before = lax.ppermute(last, axis, up)
        after = lax.ppermute(leading, axis, down)
        value = jnp.concatenate([before, value, after], axis=dim)
    return value


def forward_step(state, coeffs):
    cc = coeffs[:, 1:-1, 1:-1, :]
    spread = cc[0]
    inner = state[:, 1:-1, 1:-1, :]
    padded = jnp.pad(inner, ((0, 0), (0, 0), (0, 0), (1, 1)))
    result = (1.0 - 6.0 * spread) * inner
    result = (
        result
        + (spread - 0.5 * cc[1]) * state[:, 2:, 1:-1, :]
        + (spread + 0.5 * cc[1]) * state[:, :-2, 1:-1, :]
    )
    result = (
        result
        + (spread - 0.5 * cc[2]) * state[:, 1:-1, 2:, :]
        + (spread + 0.5 * cc[2]) * state[:, 1:-1, :-2, :]
    )
    result = (
        result
        + (spread - 0.5 * cc[3]) * padded[..., 2:]
        + (spread + 0.5 * cc[3]) * padded[..., :-2]
    )
    return result


def adjoint_step(state, coeffs):
    spread = coeffs[0]
    plus_x = (spread - 0.5 * coeffs[1]) * state
    minus_x = (spread + 0.5 * coeffs[1]) * state
    plus_y = (spread - 0.5 * coeffs[2]) * state
    minus_y = (spread + 0.5 * coeffs[2]) * state
    cc = coeffs[:, 1:-1, 1:-1, :]
    inner = state[:, 1:-1, 1:-1, :]
    pad_plus = jnp.pad((cc[0] - 0.5 * cc[3]) * inner, ((0, 0), (0, 0), (0, 0), (1, 1)))
    pad_minus = jnp.pad((cc[0] + 0.5 * cc[3]) * inner, ((0, 0), (0, 0), (0, 0), (1, 1)))
    result = (1.0 - 6.0 * cc[0]) * inner
    result = result + plus_x[:, :-2, 1:-1, :] + minus_x[:, 2:, 1:-1, :]
    result = result + plus_y[:, 1:-1, :-2, :] + minus_y[:, 1:-1, 2:, :]
    result = result + pad_plus[..., :-2] + pad_minus[..., 2:]
    return result


def factor_inverse(gram, count):
    lower = jnp.linalg.cholesky(gram)
    return jax.scipy.linalg.solve_triangular(lower, jnp.eye(count, dtype=jnp.float32), lower=True)


def shards(probes, velocity, diffusivity, obs_weight):
    group = probes.shape[0]
    count = group * lax.axis_size("probe")
    ncells = (
        probes.shape[1]
        * probes.shape[2]
        * probes.shape[3]
        * lax.axis_size("sx")
        * lax.axis_size("sy")
    )
    coeffs = jnp.concatenate([diffusivity[None], velocity], axis=0)
    highest = lax.Precision.HIGHEST
    edge_coeffs = extended(coeffs, (("sx", 1), ("sy", 2)), 1)

    def forward(state):
        for step in range(STEPS):
            padded = extended(state, (("sx", 1), ("sy", 2)), 1)
            state = forward_step(padded, edge_coeffs)
        return state

    state = obs_weight * forward(probes)
    for step in range(STEPS):
        padded = extended(state, (("sx", 1), ("sy", 2)), 1)
        state = adjoint_step(padded, edge_coeffs)
    images = state
    again = forward(images)
    root = jnp.sqrt(obs_weight) * again
    both = jnp.stack([images, root], axis=1)
    slabs = lax.all_to_all(both, "probe", split_axis=2, concat_axis=0, tiled=True)
    flat = slabs[:, 0].reshape(count, -1)
    flat_root = slabs[:, 1].reshape(count, -1)
    partial_gram = jnp.dot(flat, flat.T, precision=highest)
    partial_cross = jnp.dot(flat_root, flat_root.T, precision=highest)
    sums = lax.psum(jnp.stack([partial_gram, partial_cross]), ("probe", "sx", "sy")) / ncells
    gram, cross = (sums[0], sums[1])
    inverse = factor_inverse(gram, count)
    basis_slab = jnp.dot(inverse, flat, precision=highest)
    basis_fields = lax.all_to_all(
        basis_slab.reshape(slabs[:, 0].shape), "probe", split_axis=0, concat_axis=1, tiled=True
    )
    projected = jnp.dot(jnp.dot(inverse, cross, precision=highest), inverse.T, precision=highest)
    return (basis_fields, projected)


def solution(mesh):
    return jax.shard_map(
        shards,
        mesh=mesh,
        in_specs=(
            P("probe", "sx", "sy", None),
            P(None, "sx", "sy", None),
            P("sx", "sy", None),
            P("sx", "sy", None),
        ),
        out_specs=(P("probe", "sx", "sy", None), P()),
        check_vma=False,
    )
```

profile of v0, /device:TPU:1, one launch (start us, length us, event | category | flops | bytes accessed | tf_op | source)
XLA Modules:
  0.0 471.6 jit_solution(13638757533432052887)
XLA Ops:
  3.0 4.6 collective-permute-start.1
  7.6 3.0 copy.36
  12.0 4.4 collective-permute-start.3
  21.8 3.5 fusion.10
  26.7 4.0 collective-permute-start.5
  33.3 4.9 %collective-permute-start.7 = (f32[2,34,1,256]{3,1,2,0:T(8,128)S(1)}, f32[2,34,1,256]{3,1,2,0:T(8,128)S(1)}, u32[]{:S(2)}, u32[]{:S(2)}) collective-permute-start(f32[2,34,1,256]{3,1,2,0:T(8,128)S(1)} %get-tuple-element.46), channel_id=1, source_target_pairs={{0,1},{1,2},{2,3},{3,4},{4,5},{5,6},{6,7},{8,9},{9,10},{10,11},{11... | collective-permute-start | bytes 208904 | tf_op jit(solution)/shard_map/ppermute | solution.py:16
  38.3 4.0 collective-permute-start.16
  43.6 3.5 fusion.14
  48.4 4.6 collective-permute-start.9
  53.3 4.4 collective-permute-start.18
  60.4 4.8 %collective-permute-start.11 = (f32[2,34,1,256]{3,1,2,0:T(8,128)S(1)}, f32[2,34,1,256]{3,1,2,0:T(8,128)S(1)}, u32[]{:S(2)}, u32[]{:S(2)}) collective-permute-start(f32[2,34,1,256]{3,1,2,0:T(8,128)S(1)} %get-tuple-element.44), channel_id=1, source_target_pairs={{0,1},{1,2},{2,3},{3,4},{4,5},{5,6},{6,7},{8,9},{9,10},{10,11},{11... | collective-permute-start | bytes 208904 | tf_op jit(solution)/shard_map/ppermute | solution.py:16
  66.2 2.1 collective-permute-done.11
  68.3 3.4 fusion.18
  73.1 4.3 collective-permute-start.13
  80.0 4.4 collective-permute-start.15
  85.9 3.5 broadcast_multiply_fusion.3
  89.6 3.7 collective-permute-start.20
  98.3 4.3 collective-permute-start.22
  103.9 1.6 broadcast_multiply_fusion.7
  105.5 3.5 collective-permute-done.23
  109.5 3.9 broadcast_multiply_fusion.2
  113.5 3.5 collective-permute-start.24
  118.4 3.7 collective-permute-done.25
  122.1 4.3 collective-permute-start.26
  126.3 1.7 collective-permute-start.27
  128.1 1.6 broadcast_multiply_fusion.6
  129.7 1.9 collective-permute-done.27
  132.0 3.9 broadcast_multiply_fusion.1
  136.0 3.4 collective-permute-start.28
  140.7 3.9 collective-permute-done.29
  144.6 3.0 collective-permute-start.30
  149.4 3.5 collective-permute-done.31
  153.3 3.7 broadcast_multiply_fusion
  157.1 3.0 collective-permute-start.32
  161.4 3.7 collective-permute-done.33
  165.1 4.3 collective-permute-start.34
  171.1 3.4 collective-permute-done.35
  175.0 2.7 fusion.7
  179.1 4.0 collective-permute-start.37
  185.8 4.0 collective-permute-start.39
  189.8 2.2 collective-permute-done.39
  192.0 3.4 fusion.27
  196.8 4.0 collective-permute-start.41
  203.5 4.4 collective-permute-start.43
  207.9 2.6 collective-permute-done.43
  210.5 3.4 fusion.31
  215.3 4.4 collective-permute-start.45
  222.4 4.4 collective-permute-start.47
  228.3 3.3 fusion.35
  233.2 4.6 collective-permute-start.49
  240.4 5.3 %collective-permute-start.51 = (f32[2,34,1,256]{3,1,2,0:T(8,128)S(1)}, f32[2,34,1,256]{3,1,2,0:T(8,128)S(1)}, u32[]{:S(2)}, u32[]{:S(2)}) collective-permute-start(f32[2,34,1,256]{3,1,2,0:T(8,128)S(1)} %get-tuple-element.26), channel_id=1, source_target_pairs={{0,1},{1,2},{2,3},{3,4},{4,5},{5,6},{6,7},{8,9},{9,10},{10,11},{11... | collective-permute-start | bytes 208904 | tf_op jit(solution)/shard_map/ppermute | solution.py:16
  247.1 3.5 fusion.41
  250.9 2.4 copy.58
  253.3 79.6 %all_to_all.36 = f32[2,2,32,32,256]{4,3,0,1,2:T(8,128)S(1)} all-to-all(f32[2,2,32,32,256]{4,3,0,1,2:T(8,128)S(1)} %copy.58), channel_id=1, replica_groups=mesh['probe'=4,'sx'=4,'sy'=8] {'probe'}, dimensions={2} | all-to-all | bytes 8388608 | tf_op jit(solution)/shard_map/all_to_all | solution.py:96
  333.0 5.2 %copy.72 = f32[2,2,4,8,32,256]{5,0,2,4,3,1:T(2,128)} copy(f32[2,2,4,8,32,256]{5,4,0,1,3,2:T(8,128)S(1)} %bitcast.90) | data formatting | bytes 8388608 | tf_op jit(solution)/shard_map/all_to_all | solution.py:96
  338.2 6.1 %all_to_all.29 = f32[8,2,8,32,256]{4,0,3,2,1:T(8,128)} reshape(f32[4,2,2,8,32,256]{5,1,0,4,3,2:T(2,128)} %bitcast.91) | data formatting | bytes 8388608 | tf_op jit(solution)/shard_map/all_to_all | solution.py:96
  344.4 7.1 %fusion.131 = f32[1,8,8]{2,1,0:T(8,128)S(1)} fusion(f32[8,2,8,32,256]{4,0,3,2,1:T(8,128)} %all_to_all.29), kind=kOutput, calls=%fused_computation.253 | convolution fusion | flops 50331648 | bytes 2097408 | tf_op jit(solution)/shard_map/dot_general | solution.py:99
  351.5 7.1 %fusion.134 = f32[1,8,8]{2,1,0:T(8,128)S(1)} fusion(f32[8,2,8,32,256]{4,0,3,2,1:T(8,128)} %all_to_all.29), kind=kOutput, calls=%fused_computation.254 | convolution fusion | flops 50331648 | bytes 2097408 | tf_op jit(solution)/shard_map/dot_general | solution.py:100
  358.6 72.6 %psum.7 = f32[2,8,8]{2,1,0:T(8,128)S(1)} all-reduce(f32[2,8,8]{2,1,0:T(8,128)S(1)} %pad_maximum_fusion.117), channel_id=1, replica_groups=mesh['probe'=4,'sx'=4,'sy'=8] {'probe','sx','sy'}, use_global_device_ids=true, to_apply=%region_0.1 | all-reduce | flops 128 | bytes 1024 | tf_op jit(solution)/shard_map/psum | solution.py:101
  434.2 3.4 fusion.124
  437.6 2.0 copy.62
  439.6 4.1 all-to-all-start.1
  444.6 25.3 %all-to-all-done.1 = f32[8,8,32,256]{3,2,1,0:T(8,128)S(1)} async-done(((f32[8,8,32,256]{3,2,1,0:T(8,128)}), f32[8,8,32,256]{3,2,1,0:T(8,128)S(1)}, u32[]{:S(2)}, u32[]{:S(2)}) %all-to-all-start.1) | async-done | bytes 2097184 | tf_op jit(solution)/shard_map/all_to_all | solution.py:105
  469.9 1.5 copy.63
  (151 shorter events, 63.9 us)
Async XLA Ops:
  1.6 8.9 %collective-permute-start = (f32[2,1,32,256]{3,1,2,0:T(1,128)S(1)}, f32[2,1,32,256]{3,1,2,0:T(1,128)S(1)}, u32[]{:S(2)}, u32[]{:S(2)}) collective-permute-start(f32[2,1,32,256]{3,1,2,0:T(1,128)S(1)} %copy.38), channel_id=1, source_target_pairs={{8,0},{16,8},{24,16},{9,1},{17,9},{25,17},{10,2},{18,10},{26,18},{... | collective-permute-start | bytes 196616 | tf_op jit(solution)/shard_map/ppermute | solution.py:17
  3.0 7.6 %collective-permute-start.1 = (f32[2,1,32,256]{3,1,2,0:T(1,128)S(1)}, f32[2,1,32,256]{3,1,2,0:T(1,128)S(1)}, u32[]{:S(2)}, u32[]{:S(2)}) collective-permute-start(f32[2,1,32,256]{3,1,2,0:T(1,128)S(1)} %copy.41), channel_id=1, source_target_pairs={{0,8},{8,16},{16,24},{1,9},{9,17},{17,25},{2,10},{10,18},{18,26},{... | collective-permute-start | bytes 196616 | tf_op jit(solution)/shard_map/ppermute | solution.py:16
  7.5 8.9 %copy-start = (f32[3,32,32,256]{3,2,1,0:T(8,128)S(1)}, f32[3,32,32,256]{3,2,1,0:T(8,128)}, u32[]{:S(2)}) copy-start(f32[3,32,32,256]{3,2,1,0:T(8,128)} %param.5) | copy-start | bytes 9437188
  10.5 5.9 %copy-start.1 = (f32[32,32,256]{2,1,0:T(8,128)S(1)}, f32[32,32,256]{2,1,0:T(8,128)}, u32[]{:S(2)}) copy-start(f32[32,32,256]{2,1,0:T(8,128)} %param.6) | copy-start | bytes 3145732
  10.6 11.2 %collective-permute-start.2 = (f32[2,34,1,256]{3,1,2,0:T(8,128)S(1)}, f32[2,34,1,256]{3,1,2,0:T(8,128)S(1)}, u32[]{:S(2)}, u32[]{:S(2)}) collective-permute-start(f32[2,34,1,256]{3,1,2,0:T(8,128)S(1)} %get-tuple-element.47), channel_id=1, source_target_pairs={{1,0},{2,1},{3,2},{4,3},{5,4},{6,5},{7,6},{9,8},{10,9},{11,10},{12... | collective-permute-start | bytes 208904 | tf_op jit(solution)/shard_map/ppermute | solution.py:17
  12.0 9.8 %collective-permute-start.3 = (f32[2,34,1,256]{3,1,2,0:T(8,128)S(1)}, f32[2,34,1,256]{3,1,2,0:T(8,128)S(1)}, u32[]{:S(2)}, u32[]{:S(2)}) collective-permute-start(f32[2,34,1,256]{3,1,2,0:T(8,128)S(1)} %get-tuple-element.48), channel_id=1, source_target_pairs={{0,1},{1,2},{2,3},{3,4},{4,5},{5,6},{6,7},{8,9},{9,10},{10,11},{11... | collective-permute-start | bytes 208904 | tf_op jit(solution)/shard_map/ppermute | solution.py:16
  25.4 5.3 %collective-permute-start.4 = (f32[2,1,32,256]{3,1,2,0:T(1,128)S(1)}, f32[2,1,32,256]{3,1,2,0:T(1,128)S(1)}, u32[]{:S(2)}, u32[]{:S(2)}) collective-permute-start(f32[2,1,32,256]{3,1,2,0:T(1,128)S(1)} %get-tuple-element.70), channel_id=1, source_target_pairs={{8,0},{16,8},{24,16},{9,1},{17,9},{25,17},{10,2},{18,10},{26,18},{... | collective-permute-start | bytes 196616 | tf_op jit(solution)/shard_map/ppermute | solution.py:17
  26.7 5.3 %collective-permute-start.5 = (f32[2,1,32,256]{3,1,2,0:T(1,128)S(1)}, f32[2,1,32,256]{3,1,2,0:T(1,128)S(1)}, u32[]{:S(2)}, u32[]{:S(2)}) collective-permute-start(f32[2,1,32,256]{3,1,2,0:T(1,128)S(1)} %get-tuple-element.69), channel_id=1, source_target_pairs={{0,8},{8,16},{16,24},{1,9},{9,17},{17,25},{2,10},{10,18},{18,26},{... | collective-permute-start | bytes 196616 | tf_op jit(solution)/shard_map/ppermute | solution.py:16
  32.0 11.5 %collective-permute-start.6 = (f32[2,34,1,256]{3,1,2,0:T(8,128)S(1)}, f32[2,34,1,256]{3,1,2,0:T(8,128)S(1)}, u32[]{:S(2)}, u32[]{:S(2)}) collective-permute-start(f32[2,34,1,256]{3,1,2,0:T(8,128)S(1)} %get-tuple-element.45), channel_id=1, source_target_pairs={{1,0},{2,1},{3,2},{4,3},{5,4},{6,5},{7,6},{9,8},{10,9},{11,10},{12... | collective-permute-start | bytes 208904 | tf_op jit(solution)/shard_map/ppermute | solution.py:17
  33.3 10.2 %collective-permute-start.7 = (f32[2,34,1,256]{3,1,2,0:T(8,128)S(1)}, f32[2,34,1,256]{3,1,2,0:T(8,128)S(1)}, u32[]{:S(2)}, u32[]{:S(2)}) collective-permute-start(f32[2,34,1,256]{3,1,2,0:T(8,128)S(1)} %get-tuple-element.46), channel_id=1, source_target_pairs={{0,1},{1,2},{2,3},{3,4},{4,5},{5,6},{6,7},{8,9},{9,10},{10,11},{11... | collective-permute-start | bytes 208904 | tf_op jit(solution)/shard_map/ppermute | solution.py:16
  38.3 14.8 %collective-permute-start.16 = (f32[4,1,32,256]{3,2,1,0:T(8,128)S(1)}, f32[4,1,32,256]{3,2,1,0:T(8,128)S(1)}, u32[]{:S(2)}, u32[]{:S(2)}) collective-permute-start(f32[4,1,32,256]{3,2,1,0:T(8,128)S(1)} %get-tuple-element.17), channel_id=1, source_target_pairs={{0,8},{8,16},{16,24},{1,9},{9,17},{17,25},{2,10},{10,18},{18,26},{... | collective-permute-start | bytes 393224 | tf_op jit(solution)/shard_map/ppermute | solution.py:16
  42.3 10.8 %collective-permute-start.17 = (f32[4,1,32,256]{3,2,1,0:T(8,128)S(1)}, f32[4,1,32,256]{3,2,1,0:T(8,128)S(1)}, u32[]{:S(2)}, u32[]{:S(2)}) collective-permute-start(f32[4,1,32,256]{3,2,1,0:T(8,128)S(1)} %get-tuple-element.18), channel_id=1, source_target_pairs={{8,0},{16,8},{24,16},{9,1},{17,9},{25,17},{10,2},{18,10},{26,18},{... | collective-permute-start | bytes 393224 | tf_op jit(solution)/shard_map/ppermute | solution.py:17
  47.1 11.9 %collective-permute-start.8 = (f32[2,1,32,256]{3,1,2,0:T(1,128)S(1)}, f32[2,1,32,256]{3,1,2,0:T(1,128)S(1)}, u32[]{:S(2)}, u32[]{:S(2)}) collective-permute-start(f32[2,1,32,256]{3,1,2,0:T(1,128)S(1)} %get-tuple-element.68), channel_id=1, source_target_pairs={{8,0},{16,8},{24,16},{9,1},{17,9},{25,17},{10,2},{18,10},{26,18},{... | collective-permute-start | bytes 196616 | tf_op jit(solution)/shard_map/ppermute | solution.py:17
  48.4 10.6 %collective-permute-start.9 = (f32[2,1,32,256]{3,1,2,0:T(1,128)S(1)}, f32[2,1,32,256]{3,1,2,0:T(1,128)S(1)}, u32[]{:S(2)}, u32[]{:S(2)}) collective-permute-start(f32[2,1,32,256]{3,1,2,0:T(1,128)S(1)} %get-tuple-element.67), channel_id=1, source_target_pairs={{0,8},{8,16},{16,24},{1,9},{9,17},{17,25},{2,10},{10,18},{18,26},{... | collective-permute-start | bytes 196616 | tf_op jit(solution)/shard_map/ppermute | solution.py:16
  53.3 11.9 %copy-start.3 = (f32[32,32,256]{2,1,0:T(8,128)S(1)}, f32[32,32,256]{2,1,0:T(8,128)}, u32[]{:S(2)}) copy-start(f32[32,32,256]{2,1,0:T(8,128)} %param.7) | copy-start | bytes 3145732
  53.3 12.5 %collective-permute-start.18 = (f32[4,34,1,256]{3,1,2,0:T(8,128)S(1)}, f32[4,34,1,256]{3,1,2,0:T(8,128)S(1)}, u32[]{:S(2)}, u32[]{:S(2)}) collective-permute-start(f32[4,34,1,256]{3,1,2,0:T(8,128)S(1)} %copy.49), channel_id=1, source_target_pairs={{0,1},{1,2},{2,3},{3,4},{4,5},{5,6},{6,7},{8,9},{9,10},{10,11},{11... | collective-permute-start | bytes 417800 | tf_op jit(solution)/shard_map/ppermute | solution.py:16
  57.8 8.2 %collective-permute-start.19 = (f32[4,34,1,256]{3,1,2,0:T(8,128)S(1)}, f32[4,34,1,256]{3,1,2,0:T(8,128)S(1)}, u32[]{:S(2)}, u32[]{:S(2)}) collective-permute-start(f32[4,34,1,256]{3,1,2,0:T(8,128)S(1)} %copy.50), channel_id=1, source_target_pairs={{1,0},{2,1},{3,2},{4,3},{5,4},{6,5},{7,6},{9,8},{10,9},{11,10},{12... | collective-permute-start | bytes 417800 | tf_op jit(solution)/shard_map/ppermute | solution.py:17
  59.1 7.1 %collective-permute-start.10 = (f32[2,34,1,256]{3,1,2,0:T(8,128)S(1)}, f32[2,34,1,256]{3,1,2,0:T(8,128)S(1)}, u32[]{:S(2)}, u32[]{:S(2)}) collective-permute-start(f32[2,34,1,256]{3,1,2,0:T(8,128)S(1)} %get-tuple-element.43), channel_id=1, source_target_pairs={{1,0},{2,1},{3,2},{4,3},{5,4},{6,5},{7,6},{9,8},{10,9},{11,10},{12... | collective-permute-start | bytes 208904 | tf_op jit(solution)/shard_map/ppermute | solution.py:17
  60.4 7.9 %collective-permute-start.11 = (f32[2,34,1,256]{3,1,2,0:T(8,128)S(1)}, f32[2,34,1,256]{3,1,2,0:T(8,128)S(1)}, u32[]{:S(2)}, u32[]{:S(2)}) collective-permute-start(f32[2,34,1,256]{3,1,2,0:T(8,128)S(1)} %get-tuple-element.44), channel_id=1, source_target_pairs={{0,1},{1,2},{2,3},{3,4},{4,5},{5,6},{6,7},{8,9},{9,10},{10,11},{11... | collective-permute-start | bytes 208904 | tf_op jit(solution)/shard_map/ppermute | solution.py:16
  71.8 6.1 %collective-permute-start.12 = (f32[2,1,32,256]{3,1,2,0:T(1,128)S(1)}, f32[2,1,32,256]{3,1,2,0:T(1,128)S(1)}, u32[]{:S(2)}, u32[]{:S(2)}) collective-permute-start(f32[2,1,32,256]{3,1,2,0:T(1,128)S(1)} %get-tuple-element.66), channel_id=1, source_target_pairs={{8,0},{16,8},{24,16},{9,1},{17,9},{25,17},{10,2},{18,10},{26,18},{... | collective-permute-start | bytes 196616 | tf_op jit(solution)/shard_map/ppermute | solution.py:17
  73.1 5.6 %collective-permute-start.13 = (f32[2,1,32,256]{3,1,2,0:T(1,128)S(1)}, f32[2,1,32,256]{3,1,2,0:T(1,128)S(1)}, u32[]{:S(2)}, u32[]{:S(2)}) collective-permute-start(f32[2,1,32,256]{3,1,2,0:T(1,128)S(1)} %get-tuple-element.65), channel_id=1, source_target_pairs={{0,8},{8,16},{16,24},{1,9},{9,17},{17,25},{2,10},{10,18},{18,26},{... | collective-permute-start | bytes 196616 | tf_op jit(solution)/shard_map/ppermute | solution.py:16
  78.7 6.1 %collective-permute-start.14 = (f32[2,34,1,256]{3,1,2,0:T(8,128)S(1)}, f32[2,34,1,256]{3,1,2,0:T(8,128)S(1)}, u32[]{:S(2)}, u32[]{:S(2)}) collective-permute-start(f32[2,34,1,256]{3,1,2,0:T(8,128)S(1)} %get-tuple-element.41), channel_id=1, source_target_pairs={{1,0},{2,1},{3,2},{4,3},{5,4},{6,5},{7,6},{9,8},{10,9},{11,10},{12... | collective-permute-start | bytes 208904 | tf_op jit(solution)/shard_map/ppermute | solution.py:17
  80.0 5.9 %collective-permute-start.15 = (f32[2,34,1,256]{3,1,2,0:T(8,128)S(1)}, f32[2,34,1,256]{3,1,2,0:T(8,128)S(1)}, u32[]{:S(2)}, u32[]{:S(2)}) collective-permute-start(f32[2,34,1,256]{3,1,2,0:T(8,128)S(1)} %get-tuple-element.42), channel_id=1, source_target_pairs={{0,1},{1,2},{2,3},{3,4},{4,5},{5,6},{6,7},{8,9},{9,10},{10,11},{11... | collective-permute-start | bytes 208904 | tf_op jit(solution)/shard_map/ppermute | solution.py:16
  89.6 8.2 %collective-permute-start.20 = (f32[2,1,32,256]{3,1,2,0:T(1,128)S(1)}, f32[2,1,32,256]{3,1,2,0:T(1,128)S(1)}, u32[]{:S(2)}, u32[]{:S(2)}) collective-permute-start(f32[2,1,32,256]{3,1,2,0:T(1,128)S(1)} %get-tuple-element.63), channel_id=1, source_target_pairs={{0,8},{8,16},{16,24},{1,9},{9,17},{17,25},{2,10},{10,18},{18,26},{... | collective-permute-start | bytes 196616 | tf_op jit(solution)/shard_map/ppermute | solution.py:16
  93.3 5.0 %collective-permute-start.21 = (f32[2,1,32,256]{3,1,2,0:T(1,128)S(1)}, f32[2,1,32,256]{3,1,2,0:T(1,128)S(1)}, u32[]{:S(2)}, u32[]{:S(2)}) collective-permute-start(f32[2,1,32,256]{3,1,2,0:T(1,128)S(1)} %get-tuple-element.64), channel_id=1, source_target_pairs={{8,0},{16,8},{24,16},{9,1},{17,9},{25,17},{10,2},{18,10},{26,18},{... | collective-permute-start | bytes 196616 | tf_op jit(solution)/shard_map/ppermute | solution.py:17
  98.3 7.2 %collective-permute-start.22 = (f32[2,34,1,256]{3,1,2,0:T(8,128)S(1)}, f32[2,34,1,256]{3,1,2,0:T(8,128)S(1)}, u32[]{:S(2)}, u32[]{:S(2)}) collective-permute-start(f32[2,34,1,256]{3,1,2,0:T(8,128)S(1)} %get-tuple-element.39), channel_id=1, source_target_pairs={{0,1},{1,2},{2,3},{3,4},{4,5},{5,6},{6,7},{8,9},{9,10},{10,11},{11... | collective-permute-start | bytes 208904 | tf_op jit(solution)/shard_map/ppermute | solution.py:16
  102.6 6.4 %collective-permute-start.23 = (f32[2,34,1,256]{3,1,2,0:T(8,128)S(1)}, f32[2,34,1,256]{3,1,2,0:T(8,128)S(1)}, u32[]{:S(2)}, u32[]{:S(2)}) collective-permute-start(f32[2,34,1,256]{3,1,2,0:T(8,128)S(1)} %get-tuple-element.40), channel_id=1, source_target_pairs={{1,0},{2,1},{3,2},{4,3},{5,4},{6,5},{7,6},{9,8},{10,9},{11,10},{12... | collective-permute-start | bytes 208904 | tf_op jit(solution)/shard_map/ppermute | solution.py:17
  113.5 4.9 %collective-permute-start.24 = (f32[2,1,32,256]{3,1,2,0:T(1,128)S(1)}, f32[2,1,32,256]{3,1,2,0:T(1,128)S(1)}, u32[]{:S(2)}, u32[]{:S(2)}) collective-permute-start(f32[2,1,32,256]{3,1,2,0:T(1,128)S(1)} %get-tuple-element.61), channel_id=1, source_target_pairs={{0,8},{8,16},{16,24},{1,9},{9,17},{17,25},{2,10},{10,18},{18,26},{... | collective-permute-start | bytes 196616 | tf_op jit(solution)/shard_map/ppermute | solution.py:16
  117.0 5.0 %collective-permute-start.25 = (f32[2,1,32,256]{3,1,2,0:T(1,128)S(1)}, f32[2,1,32,256]{3,1,2,0:T(1,128)S(1)}, u32[]{:S(2)}, u32[]{:S(2)}) collective-permute-start(f32[2,1,32,256]{3,1,2,0:T(1,128)S(1)} %get-tuple-element.62), channel_id=1, source_target_pairs={{8,0},{16,8},{24,16},{9,1},{17,9},{25,17},{10,2},{18,10},{26,18},{... | collective-permute-start | bytes 196616 | tf_op jit(solution)/shard_map/ppermute | solution.py:17
  122.1 7.6 %collective-permute-start.26 = (f32[2,34,1,256]{3,1,2,0:T(8,128)S(1)}, f32[2,34,1,256]{3,1,2,0:T(8,128)S(1)}, u32[]{:S(2)}, u32[]{:S(2)}) collective-permute-start(f32[2,34,1,256]{3,1,2,0:T(8,128)S(1)} %get-tuple-element.37), channel_id=1, source_target_pairs={{0,1},{1,2},{2,3},{3,4},{4,5},{5,6},{6,7},{8,9},{9,10},{10,11},{11... | collective-permute-start | bytes 208904 | tf_op jit(solution)/shard_map/ppermute | solution.py:16
  126.3 5.2 %collective-permute-start.27 = (f32[2,34,1,256]{3,1,2,0:T(8,128)S(1)}, f32[2,34,1,256]{3,1,2,0:T(8,128)S(1)}, u32[]{:S(2)}, u32[]{:S(2)}) collective-permute-start(f32[2,34,1,256]{3,1,2,0:T(8,128)S(1)} %get-tuple-element.38), channel_id=1, source_target_pairs={{1,0},{2,1},{3,2},{4,3},{5,4},{6,5},{7,6},{9,8},{10,9},{11,10},{12... | collective-permute-start | bytes 208904 | tf_op jit(solution)/shard_map/ppermute | solution.py:17
  136.0 4.7 collective-permute-start.28
  139.4 5.2 %collective-permute-start.29 = (f32[2,1,32,256]{3,1,2,0:T(1,128)S(1)}, f32[2,1,32,256]{3,1,2,0:T(1,128)S(1)}, u32[]{:S(2)}, u32[]{:S(2)}) collective-permute-start(f32[2,1,32,256]{3,1,2,0:T(1,128)S(1)} %get-tuple-element.60), channel_id=1, source_target_pairs={{8,0},{16,8},{24,16},{9,1},{17,9},{25,17},{10,2},{18,10},{26,18},{... | collective-permute-start | bytes 196616 | tf_op jit(solution)/shard_map/ppermute | solution.py:17
  144.6 4.8 %collective-permute-start.30 = (f32[2,34,1,256]{3,1,2,0:T(8,128)S(1)}, f32[2,34,1,256]{3,1,2,0:T(8,128)S(1)}, u32[]{:S(2)}, u32[]{:S(2)}) collective-permute-start(f32[2,34,1,256]{3,1,2,0:T(8,128)S(1)} %get-tuple-element.35), channel_id=1, source_target_pairs={{0,1},{1,2},{2,3},{3,4},{4,5},{5,6},{6,7},{8,9},{9,10},{10,11},{11... | collective-permute-start | bytes 208904 | tf_op jit(solution)/shard_map/ppermute | solution.py:16
  147.7 5.2 %collective-permute-start.31 = (f32[2,34,1,256]{3,1,2,0:T(8,128)S(1)}, f32[2,34,1,256]{3,1,2,0:T(8,128)S(1)}, u32[]{:S(2)}, u32[]{:S(2)}) collective-permute-start(f32[2,34,1,256]{3,1,2,0:T(8,128)S(1)} %get-tuple-element.36), channel_id=1, source_target_pairs={{1,0},{2,1},{3,2},{4,3},{5,4},{6,5},{7,6},{9,8},{10,9},{11,10},{12... | collective-permute-start | bytes 208904 | tf_op jit(solution)/shard_map/ppermute | solution.py:17
  157.1 4.3 collective-permute-start.32
  160.1 5.0 %collective-permute-start.33 = (f32[2,1,32,256]{3,1,2,0:T(1,128)S(1)}, f32[2,1,32,256]{3,1,2,0:T(1,128)S(1)}, u32[]{:S(2)}, u32[]{:S(2)}) collective-permute-start(f32[2,1,32,256]{3,1,2,0:T(1,128)S(1)} %get-tuple-element.58), channel_id=1, source_target_pairs={{8,0},{16,8},{24,16},{9,1},{17,9},{25,17},{10,2},{18,10},{26,18},{... | collective-permute-start | bytes 196616 | tf_op jit(solution)/shard_map/ppermute | solution.py:17
  165.1 6.0 %collective-permute-start.34 = (f32[2,34,1,256]{3,1,2,0:T(8,128)S(1)}, f32[2,34,1,256]{3,1,2,0:T(8,128)S(1)}, u32[]{:S(2)}, u32[]{:S(2)}) collective-permute-start(f32[2,34,1,256]{3,1,2,0:T(8,128)S(1)} %get-tuple-element.33), channel_id=1, source_target_pairs={{0,1},{1,2},{2,3},{3,4},{4,5},{5,6},{6,7},{8,9},{9,10},{10,11},{11... | collective-permute-start | bytes 208904 | tf_op jit(solution)/shard_map/ppermute | solution.py:16
  169.4 5.2 %collective-permute-start.35 = (f32[2,34,1,256]{3,1,2,0:T(8,128)S(1)}, f32[2,34,1,256]{3,1,2,0:T(8,128)S(1)}, u32[]{:S(2)}, u32[]{:S(2)}) collective-permute-start(f32[2,34,1,256]{3,1,2,0:T(8,128)S(1)} %get-tuple-element.34), channel_id=1, source_target_pairs={{1,0},{2,1},{3,2},{4,3},{5,4},{6,5},{7,6},{9,8},{10,9},{11,10},{12... | collective-permute-start | bytes 208904 | tf_op jit(solution)/shard_map/ppermute | solution.py:17
  171.1 3.9 copy-start.2
  177.8 5.3 %collective-permute-start.36 = (f32[2,1,32,256]{3,1,2,0:T(1,128)S(1)}, f32[2,1,32,256]{3,1,2,0:T(1,128)S(1)}, u32[]{:S(2)}, u32[]{:S(2)}) collective-permute-start(f32[2,1,32,256]{3,1,2,0:T(1,128)S(1)} %get-tuple-element.56), channel_id=1, source_target_pairs={{8,0},{16,8},{24,16},{9,1},{17,9},{25,17},{10,2},{18,10},{26,18},{... | collective-permute-start | bytes 196616 | tf_op jit(solution)/shard_map/ppermute | solution.py:17
  179.1 5.3 %collective-permute-start.37 = (f32[2,1,32,256]{3,1,2,0:T(1,128)S(1)}, f32[2,1,32,256]{3,1,2,0:T(1,128)S(1)}, u32[]{:S(2)}, u32[]{:S(2)}) collective-permute-start(f32[2,1,32,256]{3,1,2,0:T(1,128)S(1)} %get-tuple-element.55), channel_id=1, source_target_pairs={{0,8},{8,16},{16,24},{1,9},{9,17},{17,25},{2,10},{10,18},{18,26},{... | collective-permute-start | bytes 196616 | tf_op jit(solution)/shard_map/ppermute | solution.py:16
  184.5 5.3 %collective-permute-start.38 = (f32[2,34,1,256]{3,1,2,0:T(8,128)S(1)}, f32[2,34,1,256]{3,1,2,0:T(8,128)S(1)}, u32[]{:S(2)}, u32[]{:S(2)}) collective-permute-start(f32[2,34,1,256]{3,1,2,0:T(8,128)S(1)} %get-tuple-element.31), channel_id=1, source_target_pairs={{1,0},{2,1},{3,2},{4,3},{5,4},{6,5},{7,6},{9,8},{10,9},{11,10},{12... | collective-permute-start | bytes 208904 | tf_op jit(solution)/shard_map/ppermute | solution.py:17
  185.8 6.2 %collective-permute-start.39 = (f32[2,34,1,256]{3,1,2,0:T(8,128)S(1)}, f32[2,34,1,256]{3,1,2,0:T(8,128)S(1)}, u32[]{:S(2)}, u32[]{:S(2)}) collective-permute-start(f32[2,34,1,256]{3,1,2,0:T(8,128)S(1)} %get-tuple-element.32), channel_id=1, source_target_pairs={{0,1},{1,2},{2,3},{3,4},{4,5},{5,6},{6,7},{8,9},{9,10},{10,11},{11... | collective-permute-start | bytes 208904 | tf_op jit(solution)/shard_map/ppermute | solution.py:16
  195.5 5.3 %collective-permute-start.40 = (f32[2,1,32,256]{3,1,2,0:T(1,128)S(1)}, f32[2,1,32,256]{3,1,2,0:T(1,128)S(1)}, u32[]{:S(2)}, u32[]{:S(2)}) collective-permute-start(f32[2,1,32,256]{3,1,2,0:T(1,128)S(1)} %get-tuple-element.54), channel_id=1, source_target_pairs={{8,0},{16,8},{24,16},{9,1},{17,9},{25,17},{10,2},{18,10},{26,18},{... | collective-permute-start | bytes 196616 | tf_op jit(solution)/shard_map/ppermute | solution.py:17
  196.8 5.3 %collective-permute-start.41 = (f32[2,1,32,256]{3,1,2,0:T(1,128)S(1)}, f32[2,1,32,256]{3,1,2,0:T(1,128)S(1)}, u32[]{:S(2)}, u32[]{:S(2)}) collective-permute-start(f32[2,1,32,256]{3,1,2,0:T(1,128)S(1)} %get-tuple-element.53), channel_id=1, source_target_pairs={{0,8},{8,16},{16,24},{1,9},{9,17},{17,25},{2,10},{10,18},{18,26},{... | collective-permute-start | bytes 196616 | tf_op jit(solution)/shard_map/ppermute | solution.py:16
  202.2 5.8 %collective-permute-start.42 = (f32[2,34,1,256]{3,1,2,0:T(8,128)S(1)}, f32[2,34,1,256]{3,1,2,0:T(8,128)S(1)}, u32[]{:S(2)}, u32[]{:S(2)}) collective-permute-start(f32[2,34,1,256]{3,1,2,0:T(8,128)S(1)} %get-tuple-element.29), channel_id=1, source_target_pairs={{1,0},{2,1},{3,2},{4,3},{5,4},{6,5},{7,6},{9,8},{10,9},{11,10},{12... | collective-permute-start | bytes 208904 | tf_op jit(solution)/shard_map/ppermute | solution.py:17
  203.5 7.0 %collective-permute-start.43 = (f32[2,34,1,256]{3,1,2,0:T(8,128)S(1)}, f32[2,34,1,256]{3,1,2,0:T(8,128)S(1)}, u32[]{:S(2)}, u32[]{:S(2)}) collective-permute-start(f32[2,34,1,256]{3,1,2,0:T(8,128)S(1)} %get-tuple-element.30), channel_id=1, source_target_pairs={{0,1},{1,2},{2,3},{3,4},{4,5},{5,6},{6,7},{8,9},{9,10},{10,11},{11... | collective-permute-start | bytes 208904 | tf_op jit(solution)/shard_map/ppermute | solution.py:16
  214.0 5.8 %collective-permute-start.44 = (f32[2,1,32,256]{3,1,2,0:T(1,128)S(1)}, f32[2,1,32,256]{3,1,2,0:T(1,128)S(1)}, u32[]{:S(2)}, u32[]{:S(2)}) collective-permute-start(f32[2,1,32,256]{3,1,2,0:T(1,128)S(1)} %get-tuple-element.52), channel_id=1, source_target_pairs={{8,0},{16,8},{24,16},{9,1},{17,9},{25,17},{10,2},{18,10},{26,18},{... | collective-permute-start | bytes 196616 | tf_op jit(solution)/shard_map/ppermute | solution.py:17
  215.3 5.8 %collective-permute-start.45 = (f32[2,1,32,256]{3,1,2,0:T(1,128)S(1)}, f32[2,1,32,256]{3,1,2,0:T(1,128)S(1)}, u32[]{:S(2)}, u32[]{:S(2)}) collective-permute-start(f32[2,1,32,256]{3,1,2,0:T(1,128)S(1)} %get-tuple-element.51), channel_id=1, source_target_pairs={{0,8},{8,16},{16,24},{1,9},{9,17},{17,25},{2,10},{10,18},{18,26},{... | collective-permute-start | bytes 196616 | tf_op jit(solution)/shard_map/ppermute | solution.py:16
  221.1 5.8 %collective-permute-start.46 = (f32[2,34,1,256]{3,1,2,0:T(8,128)S(1)}, f32[2,34,1,256]{3,1,2,0:T(8,128)S(1)}, u32[]{:S(2)}, u32[]{:S(2)}) collective-permute-start(f32[2,34,1,256]{3,1,2,0:T(8,128)S(1)} %get-tuple-element.27), channel_id=1, source_target_pairs={{1,0},{2,1},{3,2},{4,3},{5,4},{6,5},{7,6},{9,8},{10,9},{11,10},{12... | collective-permute-start | bytes 208904 | tf_op jit(solution)/shard_map/ppermute | solution.py:17
  222.4 5.9 %collective-permute-start.47 = (f32[2,34,1,256]{3,1,2,0:T(8,128)S(1)}, f32[2,34,1,256]{3,1,2,0:T(8,128)S(1)}, u32[]{:S(2)}, u32[]{:S(2)}) collective-permute-start(f32[2,34,1,256]{3,1,2,0:T(8,128)S(1)} %get-tuple-element.28), channel_id=1, source_target_pairs={{0,1},{1,2},{2,3},{3,4},{4,5},{5,6},{6,7},{8,9},{9,10},{10,11},{11... | collective-permute-start | bytes 208904 | tf_op jit(solution)/shard_map/ppermute | solution.py:16
  231.6 14.1 %copy-start.4 = (f32[32,32,256]{2,1,0:T(8,128)S(1)}, f32[32,32,256]{2,1,0:T(8,128)}, u32[]{:S(2)}) copy-start(f32[32,32,256]{2,1,0:T(8,128)} %param.7) | copy-start | bytes 3145732
  231.7 6.1 %collective-permute-start.48 = (f32[2,1,32,256]{3,1,2,0:T(1,128)S(1)}, f32[2,1,32,256]{3,1,2,0:T(1,128)S(1)}, u32[]{:S(2)}, u32[]{:S(2)}) collective-permute-start(f32[2,1,32,256]{3,1,2,0:T(1,128)S(1)} %get-tuple-element.50), channel_id=1, source_target_pairs={{8,0},{16,8},{24,16},{9,1},{17,9},{25,17},{10,2},{18,10},{26,18},{... | collective-permute-start | bytes 196616 | tf_op jit(solution)/shard_map/ppermute | solution.py:17
  233.2 5.9 %collective-permute-start.49 = (f32[2,1,32,256]{3,1,2,0:T(1,128)S(1)}, f32[2,1,32,256]{3,1,2,0:T(1,128)S(1)}, u32[]{:S(2)}, u32[]{:S(2)}) collective-permute-start(f32[2,1,32,256]{3,1,2,0:T(1,128)S(1)} %get-tuple-element.49), channel_id=1, source_target_pairs={{0,8},{8,16},{16,24},{1,9},{9,17},{17,25},{2,10},{10,18},{18,26},{... | collective-permute-start | bytes 196616 | tf_op jit(solution)/shard_map/ppermute | solution.py:16
  239.1 7.5 %collective-permute-start.50 = (f32[2,34,1,256]{3,1,2,0:T(8,128)S(1)}, f32[2,34,1,256]{3,1,2,0:T(8,128)S(1)}, u32[]{:S(2)}, u32[]{:S(2)}) collective-permute-start(f32[2,34,1,256]{3,1,2,0:T(8,128)S(1)} %get-tuple-element.25), channel_id=1, source_target_pairs={{1,0},{2,1},{3,2},{4,3},{5,4},{6,5},{7,6},{9,8},{10,9},{11,10},{12... | collective-permute-start | bytes 208904 | tf_op jit(solution)/shard_map/ppermute | solution.py:17
  240.4 6.7 %collective-permute-start.51 = (f32[2,34,1,256]{3,1,2,0:T(8,128)S(1)}, f32[2,34,1,256]{3,1,2,0:T(8,128)S(1)}, u32[]{:S(2)}, u32[]{:S(2)}) collective-permute-start(f32[2,34,1,256]{3,1,2,0:T(8,128)S(1)} %get-tuple-element.26), channel_id=1, source_target_pairs={{0,1},{1,2},{2,3},{3,4},{4,5},{5,6},{6,7},{8,9},{9,10},{10,11},{11... | collective-permute-start | bytes 208904 | tf_op jit(solution)/shard_map/ppermute | solution.py:16
  439.6 30.3 %all-to-all-start.1 = ((f32[8,8,32,256]{3,2,1,0:T(8,128)}), f32[8,8,32,256]{3,2,1,0:T(8,128)S(1)}, u32[]{:S(2)}, u32[]{:S(2)}) async-start(f32[8,8,32,256]{3,2,1,0:T(8,128)} %copy.62), calls=%async_computation.1 | async-start | bytes 4194304 | tf_op jit(solution)/shard_map/all_to_all | solution.py:105
where the time goes:
time: 481 us; the launch traced here: 472 us
  blocking collectives  152 us (32%)
  starting transfers between devices  147 us (31%)
  waiting for transfers between devices  66.8 us (14%)
  other arithmetic  53 us (11%)
  local copies, waits for them, and re-layouts  31.4 us (7%)
  matrix products  18.7 us (4%)
    ppermute x26, starting transfers between devices, extended(): before = lax.ppermute(last, axis, up)  109 us
    all_to_all x1, blocking collectives, shards(): lax.all_to_all(both, 'probe', split_axis=2, concat_axis=0, tiled=True)  79.6 us
    psum x1, blocking collectives, shards(): lax.psum(jnp.stack([partial_gram, partial_cross]), ('probe', 'sx', 'sy'))  72.6 us
    ppermute x26, starting transfers between devices, extended(): after = lax.ppermute(leading, axis, down)  34.3 us
    all_to_all x1, waiting for transfers between devices, shards(): lax.all_to_all(basis_slab.reshape(slabs[:, 0].shape), 'probe', split_axis...  25.3 us
    ppermute x26, waiting for transfers between devices, extended(): after = lax.ppermute(leading, axis, down)  24.1 us
    add x6, other arithmetic, forward_step(): result + (spread - 0.5 * cc[3]) * padded[..., 2:]  20.5 us
    ppermute x26, waiting for transfers between devices, extended(): before = lax.ppermute(last, axis, up)  17.3 us
  transfers between devices with their start and end apart: 53, of which 21 were waited for; matrix products, arithmetic and copies ran while one was open for 5% of the time, Pallas kernels for 0%

commit v1 on v0

--- a/solution.py
+++ b/solution.py
@@ -98,7 +98,9 @@
     flat_root = slabs[:, 1].reshape(count, -1)
     partial_gram = jnp.dot(flat, flat.T, precision=highest)
     partial_cross = jnp.dot(flat_root, flat_root.T, precision=highest)
-    sums = lax.psum(jnp.stack([partial_gram, partial_cross]), ("probe", "sx", "sy")) / ncells
+    sums = (
+        lax.psum(lax.psum(jnp.stack([partial_gram, partial_cross]), ("sx", "sy")), "probe") / ncells
+    )
     gram, cross = (sums[0], sums[1])
     inverse = factor_inverse(gram, count)
     basis_slab = jnp.dot(inverse, flat, precision=highest)

time: 481 us -> 506 us (1.052)
  blocking collectives: 152 us -> 178 us
    psum x1 -> x2, blocking collectives: 72.6 us -> 98 us  [the longest x1 76.1 us: shards(): lax.psum(jnp.stack([partial_gram, partial_cross]), ('sx', 'sy'))]
where the time goes in v1:
time: 506 us; the launch traced here: 497 us
  blocking collectives  178 us (35%)
  starting transfers between devices  148 us (29%)
  waiting for transfers between devices  66.8 us (13%)
  other arithmetic  53 us (10%)
  local copies, waits for them, and re-layouts  31.4 us (6%)
  matrix products  18.7 us (4%)
    ppermute x26, starting transfers between devices, extended(): before = lax.ppermute(last, axis, up)  109 us
    all_to_all x1, blocking collectives, shards(): lax.all_to_all(both, 'probe', split_axis=2, concat_axis=0, tiled=True)  79.6 us
    psum x1, blocking collectives, shards(): lax.psum(jnp.stack([partial_gram, partial_cross]), ('sx', 'sy'))  76.1 us
    ppermute x26, starting transfers between devices, extended(): after = lax.ppermute(leading, axis, down)  34.3 us
    all_to_all x1, waiting for transfers between devices, shards(): lax.all_to_all(basis_slab.reshape(slabs[:, 0].shape), 'probe', split_axis...  25.3 us
    ppermute x26, waiting for transfers between devices, extended(): after = lax.ppermute(leading, axis, down)  24.1 us
    psum x1, blocking collectives, shards(): lax.psum(lax.psum(jnp.stack([partial_gram, partial_cross]), ('sx', 'sy'))...  21.9 us
    add x6, other arithmetic, forward_step(): result + (spread - 0.5 * cc[3]) * padded[..., 2:]  20.5 us
  transfers between devices with their start and end apart: 53, of which 21 were waited for; matrix products, arithmetic and copies ran while one was open for 5% of the time, Pallas kernels for 0%

profile of v1, /device:TPU:1, one launch (start us, length us, event | category | flops | bytes accessed | tf_op | source)
XLA Modules:
  0.0 497.1 jit_solution(6168275862018047172)
XLA Ops:
  3.0 4.6 collective-permute-start.1
  7.6 3.0 copy.36
  12.0 4.4 collective-permute-start.3
  21.8 3.5 fusion.10
  26.7 4.0 collective-permute-start.5
  33.3 4.9 collective-permute-start.7
  38.3 4.0 collective-permute-start.16
  43.6 3.5 fusion.14
  48.4 4.6 collective-permute-start.9
  53.3 4.4 collective-permute-start.18
  60.4 4.8 collective-permute-start.11
  66.2 2.1 collective-permute-done.11
  68.3 3.4 fusion.18
  73.1 4.3 collective-permute-start.13
  80.0 4.4 collective-permute-start.15
  85.9 3.5 broadcast_multiply_fusion.3
  89.6 3.7 collective-permute-start.20
  98.3 4.3 collective-permute-start.22
  103.9 1.6 broadcast_multiply_fusion.7
  105.5 3.5 collective-permute-done.23
  109.5 3.9 broadcast_multiply_fusion.2
  113.5 3.5 collective-permute-start.24
  118.4 3.7 collective-permute-done.25
  122.1 4.3 collective-permute-start.26
  126.3 1.7 collective-permute-start.27
  128.1 1.6 broadcast_multiply_fusion.6
  129.7 1.9 collective-permute-done.27
  132.0 3.9 broadcast_multiply_fusion.1
  136.0 3.4 collective-permute-start.28
  140.7 3.9 collective-permute-done.29
  144.6 3.0 collective-permute-start.30
  149.4 3.5 collective-permute-done.31
  153.3 3.7 broadcast_multiply_fusion
  157.1 3.0 collective-permute-start.32
  161.4 3.7 collective-permute-done.33
  165.1 4.3 collective-permute-start.34
  171.1 3.4 collective-permute-done.35
  175.0 2.7 fusion.7
  179.1 4.0 collective-permute-start.37
  185.8 4.0 collective-permute-start.39
  189.8 2.2 collective-permute-done.39
  192.0 3.4 fusion.27
  196.8 4.0 collective-permute-start.41
  203.5 4.4 collective-permute-start.43
  207.9 2.6 collective-permute-done.43
  210.5 3.4 fusion.31
  215.3 4.4 collective-permute-start.45
  222.4 4.4 collective-permute-start.47
  228.3 3.3 fusion.35
  233.2 4.6 collective-permute-start.49
  240.4 5.3 %collective-permute-start.51 = (f32[2,34,1,256]{3,1,2,0:T(8,128)S(1)}, f32[2,34,1,256]{3,1,2,0:T(8,128)S(1)}, u32[]{:S(2)}, u32[]{:S(2)}) collective-permute-start(f32[2,34,1,256]{3,1,2,0:T(8,128)S(1)} %get-tuple-element.26), channel_id=1, source_target_pairs={{0,1},{1,2},{2,3},{3,4},{4,5},{5,6},{6,7},{8,9},{9,10},{10,11},{11... | collective-permute-start | bytes 208904 | tf_op jit(solution)/shard_map/ppermute | solution.py:16
  247.1 3.5 fusion.41
  250.9 2.4 copy.58
  253.3 79.6 %all_to_all.36 = f32[2,2,32,32,256]{4,3,0,1,2:T(8,128)S(1)} all-to-all(f32[2,2,32,32,256]{4,3,0,1,2:T(8,128)S(1)} %copy.58), channel_id=1, replica_groups=mesh['probe'=4,'sx'=4,'sy'=8] {'probe'}, dimensions={2} | all-to-all | bytes 8388608 | tf_op jit(solution)/shard_map/all_to_all | solution.py:96
  333.0 5.2 %copy.72 = f32[2,2,4,8,32,256]{5,0,2,4,3,1:T(2,128)} copy(f32[2,2,4,8,32,256]{5,4,0,1,3,2:T(8,128)S(1)} %bitcast.90) | data formatting | bytes 8388608 | tf_op jit(solution)/shard_map/all_to_all | solution.py:96
  338.2 6.1 %all_to_all.29 = f32[8,2,8,32,256]{4,0,3,2,1:T(8,128)} reshape(f32[4,2,2,8,32,256]{5,1,0,4,3,2:T(2,128)} %bitcast.91) | data formatting | bytes 8388608 | tf_op jit(solution)/shard_map/all_to_all | solution.py:96
  344.4 7.1 %fusion.131 = f32[1,8,8]{2,1,0:T(8,128)S(1)} fusion(f32[8,2,8,32,256]{4,0,3,2,1:T(8,128)} %all_to_all.29), kind=kOutput, calls=%fused_computation.253 | convolution fusion | flops 50331648 | bytes 2097408 | tf_op jit(solution)/shard_map/dot_general | solution.py:99
  351.5 7.1 %fusion.134 = f32[1,8,8]{2,1,0:T(8,128)S(1)} fusion(f32[8,2,8,32,256]{4,0,3,2,1:T(8,128)} %all_to_all.29), kind=kOutput, calls=%fused_computation.254 | convolution fusion | flops 50331648 | bytes 2097408 | tf_op jit(solution)/shard_map/dot_general | solution.py:100
  358.6 76.1 %psum.14 = f32[2,8,8]{2,1,0:T(8,128)S(1)} all-reduce(f32[2,8,8]{2,1,0:T(8,128)S(1)} %pad_maximum_fusion.117), channel_id=1, replica_groups=mesh['probe'=4,'sx'=4,'sy'=8] {'sx','sy'}, use_global_device_ids=true, to_apply=%region_0.1 | all-reduce | flops 128 | bytes 1024 | tf_op jit(solution)/shard_map/psum | solution.py:102
  434.7 21.9 %psum.15 = f32[2,8,8]{2,1,0:T(8,128)S(1)} all-reduce(f32[2,8,8]{2,1,0:T(8,128)S(1)} %psum.14), channel_id=1, replica_groups=mesh['probe'=4,'sx'=4,'sy'=8] {'probe'}, use_global_device_ids=true, to_apply=%region_1.2 | all-reduce | flops 128 | bytes 1024 | tf_op jit(solution)/shard_map/psum | solution.py:102
  459.6 3.4 fusion.124
  463.0 2.0 copy.62
  465.0 4.3 all-to-all-start.1
  470.1 25.3 %all-to-all-done.1 = f32[8,8,32,256]{3,2,1,0:T(8,128)S(1)} async-done(((f32[8,8,32,256]{3,2,1,0:T(8,128)}), f32[8,8,32,256]{3,2,1,0:T(8,128)S(1)}, u32[]{:S(2)}, u32[]{:S(2)}) %all-to-all-start.1) | async-done | bytes 2097184 | tf_op jit(solution)/shard_map/all_to_all | solution.py:107
  (152 shorter events, 65.4 us)
Async XLA Ops:
  1.6 8.9 %collective-permute-start = (f32[2,1,32,256]{3,1,2,0:T(1,128)S(1)}, f32[2,1,32,256]{3,1,2,0:T(1,128)S(1)}, u32[]{:S(2)}, u32[]{:S(2)}) collective-permute-start(f32[2,1,32,256]{3,1,2,0:T(1,128)S(1)} %copy.38), channel_id=1, source_target_pairs={{8,0},{16,8},{24,16},{9,1},{17,9},{25,17},{10,2},{18,10},{26,18},{... | collective-permute-start | bytes 196616 | tf_op jit(solution)/shard_map/ppermute | solution.py:17
  3.0 7.6 %collective-permute-start.1 = (f32[2,1,32,256]{3,1,2,0:T(1,128)S(1)}, f32[2,1,32,256]{3,1,2,0:T(1,128)S(1)}, u32[]{:S(2)}, u32[]{:S(2)}) collective-permute-start(f32[2,1,32,256]{3,1,2,0:T(1,128)S(1)} %copy.41), channel_id=1, source_target_pairs={{0,8},{8,16},{16,24},{1,9},{9,17},{17,25},{2,10},{10,18},{18,26},{... | collective-permute-start | bytes 196616 | tf_op jit(solution)/shard_map/ppermute | solution.py:16
  7.5 8.9 %copy-start = (f32[3,32,32,256]{3,2,1,0:T(8,128)S(1)}, f32[3,32,32,256]{3,2,1,0:T(8,128)}, u32[]{:S(2)}) copy-start(f32[3,32,32,256]{3,2,1,0:T(8,128)} %param.5) | copy-start | bytes 9437188
  10.5 5.9 %copy-start.1 = (f32[32,32,256]{2,1,0:T(8,128)S(1)}, f32[32,32,256]{2,1,0:T(8,128)}, u32[]{:S(2)}) copy-start(f32[32,32,256]{2,1,0:T(8,128)} %param.6) | copy-start | bytes 3145732
  10.6 11.2 %collective-permute-start.2 = (f32[2,34,1,256]{3,1,2,0:T(8,128)S(1)}, f32[2,34,1,256]{3,1,2,0:T(8,128)S(1)}, u32[]{:S(2)}, u32[]{:S(2)}) collective-permute-start(f32[2,34,1,256]{3,1,2,0:T(8,128)S(1)} %get-tuple-element.47), channel_id=1, source_target_pairs={{1,0},{2,1},{3,2},{4,3},{5,4},{6,5},{7,6},{9,8},{10,9},{11,10},{12... | collective-permute-start | bytes 208904 | tf_op jit(solution)/shard_map/ppermute | solution.py:17
  12.0 9.8 %collective-permute-start.3 = (f32[2,34,1,256]{3,1,2,0:T(8,128)S(1)}, f32[2,34,1,256]{3,1,2,0:T(8,128)S(1)}, u32[]{:S(2)}, u32[]{:S(2)}) collective-permute-start(f32[2,34,1,256]{3,1,2,0:T(8,128)S(1)} %get-tuple-element.48), channel_id=1, source_target_pairs={{0,1},{1,2},{2,3},{3,4},{4,5},{5,6},{6,7},{8,9},{9,10},{10,11},{11... | collective-permute-start | bytes 208904 | tf_op jit(solution)/shard_map/ppermute | solution.py:16
  25.4 5.3 %collective-permute-start.4 = (f32[2,1,32,256]{3,1,2,0:T(1,128)S(1)}, f32[2,1,32,256]{3,1,2,0:T(1,128)S(1)}, u32[]{:S(2)}, u32[]{:S(2)}) collective-permute-start(f32[2,1,32,256]{3,1,2,0:T(1,128)S(1)} %get-tuple-element.70), channel_id=1, source_target_pairs={{8,0},{16,8},{24,16},{9,1},{17,9},{25,17},{10,2},{18,10},{26,18},{... | collective-permute-start | bytes 196616 | tf_op jit(solution)/shard_map/ppermute | solution.py:17
  26.7 5.3 %collective-permute-start.5 = (f32[2,1,32,256]{3,1,2,0:T(1,128)S(1)}, f32[2,1,32,256]{3,1,2,0:T(1,128)S(1)}, u32[]{:S(2)}, u32[]{:S(2)}) collective-permute-start(f32[2,1,32,256]{3,1,2,0:T(1,128)S(1)} %get-tuple-element.69), channel_id=1, source_target_pairs={{0,8},{8,16},{16,24},{1,9},{9,17},{17,25},{2,10},{10,18},{18,26},{... | collective-permute-start | bytes 196616 | tf_op jit(solution)/shard_map/ppermute | solution.py:16
  32.0 11.5 %collective-permute-start.6 = (f32[2,34,1,256]{3,1,2,0:T(8,128)S(1)}, f32[2,34,1,256]{3,1,2,0:T(8,128)S(1)}, u32[]{:S(2)}, u32[]{:S(2)}) collective-permute-start(f32[2,34,1,256]{3,1,2,0:T(8,128)S(1)} %get-tuple-element.45), channel_id=1, source_target_pairs={{1,0},{2,1},{3,2},{4,3},{5,4},{6,5},{7,6},{9,8},{10,9},{11,10},{12... | collective-permute-start | bytes 208904 | tf_op jit(solution)/shard_map/ppermute | solution.py:17
  33.3 10.2 %collective-permute-start.7 = (f32[2,34,1,256]{3,1,2,0:T(8,128)S(1)}, f32[2,34,1,256]{3,1,2,0:T(8,128)S(1)}, u32[]{:S(2)}, u32[]{:S(2)}) collective-permute-start(f32[2,34,1,256]{3,1,2,0:T(8,128)S(1)} %get-tuple-element.46), channel_id=1, source_target_pairs={{0,1},{1,2},{2,3},{3,4},{4,5},{5,6},{6,7},{8,9},{9,10},{10,11},{11... | collective-permute-start | bytes 208904 | tf_op jit(solution)/shard_map/ppermute | solution.py:16
  38.3 14.8 %collective-permute-start.16 = (f32[4,1,32,256]{3,2,1,0:T(8,128)S(1)}, f32[4,1,32,256]{3,2,1,0:T(8,128)S(1)}, u32[]{:S(2)}, u32[]{:S(2)}) collective-permute-start(f32[4,1,32,256]{3,2,1,0:T(8,128)S(1)} %get-tuple-element.17), channel_id=1, source_target_pairs={{0,8},{8,16},{16,24},{1,9},{9,17},{17,25},{2,10},{10,18},{18,26},{... | collective-permute-start | bytes 393224 | tf_op jit(solution)/shard_map/ppermute | solution.py:16
  42.3 10.8 %collective-permute-start.17 = (f32[4,1,32,256]{3,2,1,0:T(8,128)S(1)}, f32[4,1,32,256]{3,2,1,0:T(8,128)S(1)}, u32[]{:S(2)}, u32[]{:S(2)}) collective-permute-start(f32[4,1,32,256]{3,2,1,0:T(8,128)S(1)} %get-tuple-element.18), channel_id=1, source_target_pairs={{8,0},{16,8},{24,16},{9,1},{17,9},{25,17},{10,2},{18,10},{26,18},{... | collective-permute-start | bytes 393224 | tf_op jit(solution)/shard_map/ppermute | solution.py:17
  47.1 11.9 %collective-permute-start.8 = (f32[2,1,32,256]{3,1,2,0:T(1,128)S(1)}, f32[2,1,32,256]{3,1,2,0:T(1,128)S(1)}, u32[]{:S(2)}, u32[]{:S(2)}) collective-permute-start(f32[2,1,32,256]{3,1,2,0:T(1,128)S(1)} %get-tuple-element.68), channel_id=1, source_target_pairs={{8,0},{16,8},{24,16},{9,1},{17,9},{25,17},{10,2},{18,10},{26,18},{... | collective-permute-start | bytes 196616 | tf_op jit(solution)/shard_map/ppermute | solution.py:17
  48.4 10.6 %collective-permute-start.9 = (f32[2,1,32,256]{3,1,2,0:T(1,128)S(1)}, f32[2,1,32,256]{3,1,2,0:T(1,128)S(1)}, u32[]{:S(2)}, u32[]{:S(2)}) collective-permute-start(f32[2,1,32,256]{3,1,2,0:T(1,128)S(1)} %get-tuple-element.67), channel_id=1, source_target_pairs={{0,8},{8,16},{16,24},{1,9},{9,17},{17,25},{2,10},{10,18},{18,26},{... | collective-permute-start | bytes 196616 | tf_op jit(solution)/shard_map/ppermute | solution.py:16
  53.3 11.9 %copy-start.3 = (f32[32,32,256]{2,1,0:T(8,128)S(1)}, f32[32,32,256]{2,1,0:T(8,128)}, u32[]{:S(2)}) copy-start(f32[32,32,256]{2,1,0:T(8,128)} %param.7) | copy-start | bytes 3145732
  53.3 12.5 %collective-permute-start.18 = (f32[4,34,1,256]{3,1,2,0:T(8,128)S(1)}, f32[4,34,1,256]{3,1,2,0:T(8,128)S(1)}, u32[]{:S(2)}, u32[]{:S(2)}) collective-permute-start(f32[4,34,1,256]{3,1,2,0:T(8,128)S(1)} %copy.49), channel_id=1, source_target_pairs={{0,1},{1,2},{2,3},{3,4},{4,5},{5,6},{6,7},{8,9},{9,10},{10,11},{11... | collective-permute-start | bytes 417800 | tf_op jit(solution)/shard_map/ppermute | solution.py:16
  57.8 8.2 %collective-permute-start.19 = (f32[4,34,1,256]{3,1,2,0:T(8,128)S(1)}, f32[4,34,1,256]{3,1,2,0:T(8,128)S(1)}, u32[]{:S(2)}, u32[]{:S(2)}) collective-permute-start(f32[4,34,1,256]{3,1,2,0:T(8,128)S(1)} %copy.50), channel_id=1, source_target_pairs={{1,0},{2,1},{3,2},{4,3},{5,4},{6,5},{7,6},{9,8},{10,9},{11,10},{12... | collective-permute-start | bytes 417800 | tf_op jit(solution)/shard_map/ppermute | solution.py:17
  59.1 7.1 %collective-permute-start.10 = (f32[2,34,1,256]{3,1,2,0:T(8,128)S(1)}, f32[2,34,1,256]{3,1,2,0:T(8,128)S(1)}, u32[]{:S(2)}, u32[]{:S(2)}) collective-permute-start(f32[2,34,1,256]{3,1,2,0:T(8,128)S(1)} %get-tuple-element.43), channel_id=1, source_target_pairs={{1,0},{2,1},{3,2},{4,3},{5,4},{6,5},{7,6},{9,8},{10,9},{11,10},{12... | collective-permute-start | bytes 208904 | tf_op jit(solution)/shard_map/ppermute | solution.py:17
  60.4 7.9 %collective-permute-start.11 = (f32[2,34,1,256]{3,1,2,0:T(8,128)S(1)}, f32[2,34,1,256]{3,1,2,0:T(8,128)S(1)}, u32[]{:S(2)}, u32[]{:S(2)}) collective-permute-start(f32[2,34,1,256]{3,1,2,0:T(8,128)S(1)} %get-tuple-element.44), channel_id=1, source_target_pairs={{0,1},{1,2},{2,3},{3,4},{4,5},{5,6},{6,7},{8,9},{9,10},{10,11},{11... | collective-permute-start | bytes 208904 | tf_op jit(solution)/shard_map/ppermute | solution.py:16
  71.8 6.1 %collective-permute-start.12 = (f32[2,1,32,256]{3,1,2,0:T(1,128)S(1)}, f32[2,1,32,256]{3,1,2,0:T(1,128)S(1)}, u32[]{:S(2)}, u32[]{:S(2)}) collective-permute-start(f32[2,1,32,256]{3,1,2,0:T(1,128)S(1)} %get-tuple-element.66), channel_id=1, source_target_pairs={{8,0},{16,8},{24,16},{9,1},{17,9},{25,17},{10,2},{18,10},{26,18},{... | collective-permute-start | bytes 196616 | tf_op jit(solution)/shard_map/ppermute | solution.py:17
  73.1 5.6 %collective-permute-start.13 = (f32[2,1,32,256]{3,1,2,0:T(1,128)S(1)}, f32[2,1,32,256]{3,1,2,0:T(1,128)S(1)}, u32[]{:S(2)}, u32[]{:S(2)}) collective-permute-start(f32[2,1,32,256]{3,1,2,0:T(1,128)S(1)} %get-tuple-element.65), channel_id=1, source_target_pairs={{0,8},{8,16},{16,24},{1,9},{9,17},{17,25},{2,10},{10,18},{18,26},{... | collective-permute-start | bytes 196616 | tf_op jit(solution)/shard_map/ppermute | solution.py:16
  78.7 6.1 %collective-permute-start.14 = (f32[2,34,1,256]{3,1,2,0:T(8,128)S(1)}, f32[2,34,1,256]{3,1,2,0:T(8,128)S(1)}, u32[]{:S(2)}, u32[]{:S(2)}) collective-permute-start(f32[2,34,1,256]{3,1,2,0:T(8,128)S(1)} %get-tuple-element.41), channel_id=1, source_target_pairs={{1,0},{2,1},{3,2},{4,3},{5,4},{6,5},{7,6},{9,8},{10,9},{11,10},{12... | collective-permute-start | bytes 208904 | tf_op jit(solution)/shard_map/ppermute | solution.py:17
  80.0 5.9 %collective-permute-start.15 = (f32[2,34,1,256]{3,1,2,0:T(8,128)S(1)}, f32[2,34,1,256]{3,1,2,0:T(8,128)S(1)}, u32[]{:S(2)}, u32[]{:S(2)}) collective-permute-start(f32[2,34,1,256]{3,1,2,0:T(8,128)S(1)} %get-tuple-element.42), channel_id=1, source_target_pairs={{0,1},{1,2},{2,3},{3,4},{4,5},{5,6},{6,7},{8,9},{9,10},{10,11},{11... | collective-permute-start | bytes 208904 | tf_op jit(solution)/shard_map/ppermute | solution.py:16
  89.6 8.2 %collective-permute-start.20 = (f32[2,1,32,256]{3,1,2,0:T(1,128)S(1)}, f32[2,1,32,256]{3,1,2,0:T(1,128)S(1)}, u32[]{:S(2)}, u32[]{:S(2)}) collective-permute-start(f32[2,1,32,256]{3,1,2,0:T(1,128)S(1)} %get-tuple-element.63), channel_id=1, source_target_pairs={{0,8},{8,16},{16,24},{1,9},{9,17},{17,25},{2,10},{10,18},{18,26},{... | collective-permute-start | bytes 196616 | tf_op jit(solution)/shard_map/ppermute | solution.py:16
  93.3 5.0 %collective-permute-start.21 = (f32[2,1,32,256]{3,1,2,0:T(1,128)S(1)}, f32[2,1,32,256]{3,1,2,0:T(1,128)S(1)}, u32[]{:S(2)}, u32[]{:S(2)}) collective-permute-start(f32[2,1,32,256]{3,1,2,0:T(1,128)S(1)} %get-tuple-element.64), channel_id=1, source_target_pairs={{8,0},{16,8},{24,16},{9,1},{17,9},{25,17},{10,2},{18,10},{26,18},{... | collective-permute-start | bytes 196616 | tf_op jit(solution)/shard_map/ppermute | solution.py:17
  98.3 7.2 %collective-permute-start.22 = (f32[2,34,1,256]{3,1,2,0:T(8,128)S(1)}, f32[2,34,1,256]{3,1,2,0:T(8,128)S(1)}, u32[]{:S(2)}, u32[]{:S(2)}) collective-permute-start(f32[2,34,1,256]{3,1,2,0:T(8,128)S(1)} %get-tuple-element.39), channel_id=1, source_target_pairs={{0,1},{1,2},{2,3},{3,4},{4,5},{5,6},{6,7},{8,9},{9,10},{10,11},{11... | collective-permute-start | bytes 208904 | tf_op jit(solution)/shard_map/ppermute | solution.py:16
  102.6 6.4 %collective-permute-start.23 = (f32[2,34,1,256]{3,1,2,0:T(8,128)S(1)}, f32[2,34,1,256]{3,1,2,0:T(8,128)S(1)}, u32[]{:S(2)}, u32[]{:S(2)}) collective-permute-start(f32[2,34,1,256]{3,1,2,0:T(8,128)S(1)} %get-tuple-element.40), channel_id=1, source_target_pairs={{1,0},{2,1},{3,2},{4,3},{5,4},{6,5},{7,6},{9,8},{10,9},{11,10},{12... | collective-permute-start | bytes 208904 | tf_op jit(solution)/shard_map/ppermute | solution.py:17
  113.5 4.9 collective-permute-start.24
  117.0 5.0 %collective-permute-start.25 = (f32[2,1,32,256]{3,1,2,0:T(1,128)S(1)}, f32[2,1,32,256]{3,1,2,0:T(1,128)S(1)}, u32[]{:S(2)}, u32[]{:S(2)}) collective-permute-start(f32[2,1,32,256]{3,1,2,0:T(1,128)S(1)} %get-tuple-element.62), channel_id=1, source_target_pairs={{8,0},{16,8},{24,16},{9,1},{17,9},{25,17},{10,2},{18,10},{26,18},{... | collective-permute-start | bytes 196616 | tf_op jit(solution)/shard_map/ppermute | solution.py:17
  122.1 7.6 %collective-permute-start.26 = (f32[2,34,1,256]{3,1,2,0:T(8,128)S(1)}, f32[2,34,1,256]{3,1,2,0:T(8,128)S(1)}, u32[]{:S(2)}, u32[]{:S(2)}) collective-permute-start(f32[2,34,1,256]{3,1,2,0:T(8,128)S(1)} %get-tuple-element.37), channel_id=1, source_target_pairs={{0,1},{1,2},{2,3},{3,4},{4,5},{5,6},{6,7},{8,9},{9,10},{10,11},{11... | collective-permute-start | bytes 208904 | tf_op jit(solution)/shard_map/ppermute | solution.py:16
  126.3 5.2 %collective-permute-start.27 = (f32[2,34,1,256]{3,1,2,0:T(8,128)S(1)}, f32[2,34,1,256]{3,1,2,0:T(8,128)S(1)}, u32[]{:S(2)}, u32[]{:S(2)}) collective-permute-start(f32[2,34,1,256]{3,1,2,0:T(8,128)S(1)} %get-tuple-element.38), channel_id=1, source_target_pairs={{1,0},{2,1},{3,2},{4,3},{5,4},{6,5},{7,6},{9,8},{10,9},{11,10},{12... | collective-permute-start | bytes 208904 | tf_op jit(solution)/shard_map/ppermute | solution.py:17
  136.0 4.7 collective-permute-start.28
  139.4 5.2 %collective-permute-start.29 = (f32[2,1,32,256]{3,1,2,0:T(1,128)S(1)}, f32[2,1,32,256]{3,1,2,0:T(1,128)S(1)}, u32[]{:S(2)}, u32[]{:S(2)}) collective-permute-start(f32[2,1,32,256]{3,1,2,0:T(1,128)S(1)} %get-tuple-element.60), channel_id=1, source_target_pairs={{8,0},{16,8},{24,16},{9,1},{17,9},{25,17},{10,2},{18,10},{26,18},{... | collective-permute-start | bytes 196616 | tf_op jit(solution)/shard_map/ppermute | solution.py:17
  144.6 4.8 collective-permute-start.30
  147.7 5.2 %collective-permute-start.31 = (f32[2,34,1,256]{3,1,2,0:T(8,128)S(1)}, f32[2,34,1,256]{3,1,2,0:T(8,128)S(1)}, u32[]{:S(2)}, u32[]{:S(2)}) collective-permute-start(f32[2,34,1,256]{3,1,2,0:T(8,128)S(1)} %get-tuple-element.36), channel_id=1, source_target_pairs={{1,0},{2,1},{3,2},{4,3},{5,4},{6,5},{7,6},{9,8},{10,9},{11,10},{12... | collective-permute-start | bytes 208904 | tf_op jit(solution)/shard_map/ppermute | solution.py:17
  157.1 4.3 collective-permute-start.32
  160.1 5.0 %collective-permute-start.33 = (f32[2,1,32,256]{3,1,2,0:T(1,128)S(1)}, f32[2,1,32,256]{3,1,2,0:T(1,128)S(1)}, u32[]{:S(2)}, u32[]{:S(2)}) collective-permute-start(f32[2,1,32,256]{3,1,2,0:T(1,128)S(1)} %get-tuple-element.58), channel_id=1, source_target_pairs={{8,0},{16,8},{24,16},{9,1},{17,9},{25,17},{10,2},{18,10},{26,18},{... | collective-permute-start | bytes 196616 | tf_op jit(solution)/shard_map/ppermute | solution.py:17
  165.1 6.0 %collective-permute-start.34 = (f32[2,34,1,256]{3,1,2,0:T(8,128)S(1)}, f32[2,34,1,256]{3,1,2,0:T(8,128)S(1)}, u32[]{:S(2)}, u32[]{:S(2)}) collective-permute-start(f32[2,34,1,256]{3,1,2,0:T(8,128)S(1)} %get-tuple-element.33), channel_id=1, source_target_pairs={{0,1},{1,2},{2,3},{3,4},{4,5},{5,6},{6,7},{8,9},{9,10},{10,11},{11... | collective-permute-start | bytes 208904 | tf_op jit(solution)/shard_map/ppermute | solution.py:16
  169.4 5.2 %collective-permute-start.35 = (f32[2,34,1,256]{3,1,2,0:T(8,128)S(1)}, f32[2,34,1,256]{3,1,2,0:T(8,128)S(1)}, u32[]{:S(2)}, u32[]{:S(2)}) collective-permute-start(f32[2,34,1,256]{3,1,2,0:T(8,128)S(1)} %get-tuple-element.34), channel_id=1, source_target_pairs={{1,0},{2,1},{3,2},{4,3},{5,4},{6,5},{7,6},{9,8},{10,9},{11,10},{12... | collective-permute-start | bytes 208904 | tf_op jit(solution)/shard_map/ppermute | solution.py:17
  171.1 3.9 copy-start.2
  177.8 5.3 %collective-permute-start.36 = (f32[2,1,32,256]{3,1,2,0:T(1,128)S(1)}, f32[2,1,32,256]{3,1,2,0:T(1,128)S(1)}, u32[]{:S(2)}, u32[]{:S(2)}) collective-permute-start(f32[2,1,32,256]{3,1,2,0:T(1,128)S(1)} %get-tuple-element.56), channel_id=1, source_target_pairs={{8,0},{16,8},{24,16},{9,1},{17,9},{25,17},{10,2},{18,10},{26,18},{... | collective-permute-start | bytes 196616 | tf_op jit(solution)/shard_map/ppermute | solution.py:17
  179.1 5.3 %collective-permute-start.37 = (f32[2,1,32,256]{3,1,2,0:T(1,128)S(1)}, f32[2,1,32,256]{3,1,2,0:T(1,128)S(1)}, u32[]{:S(2)}, u32[]{:S(2)}) collective-permute-start(f32[2,1,32,256]{3,1,2,0:T(1,128)S(1)} %get-tuple-element.55), channel_id=1, source_target_pairs={{0,8},{8,16},{16,24},{1,9},{9,17},{17,25},{2,10},{10,18},{18,26},{... | collective-permute-start | bytes 196616 | tf_op jit(solution)/shard_map/ppermute | solution.py:16
  184.5 5.3 %collective-permute-start.38 = (f32[2,34,1,256]{3,1,2,0:T(8,128)S(1)}, f32[2,34,1,256]{3,1,2,0:T(8,128)S(1)}, u32[]{:S(2)}, u32[]{:S(2)}) collective-permute-start(f32[2,34,1,256]{3,1,2,0:T(8,128)S(1)} %get-tuple-element.31), channel_id=1, source_target_pairs={{1,0},{2,1},{3,2},{4,3},{5,4},{6,5},{7,6},{9,8},{10,9},{11,10},{12... | collective-permute-start | bytes 208904 | tf_op jit(solution)/shard_map/ppermute | solution.py:17
  185.8 6.2 %collective-permute-start.39 = (f32[2,34,1,256]{3,1,2,0:T(8,128)S(1)}, f32[2,34,1,256]{3,1,2,0:T(8,128)S(1)}, u32[]{:S(2)}, u32[]{:S(2)}) collective-permute-start(f32[2,34,1,256]{3,1,2,0:T(8,128)S(1)} %get-tuple-element.32), channel_id=1, source_target_pairs={{0,1},{1,2},{2,3},{3,4},{4,5},{5,6},{6,7},{8,9},{9,10},{10,11},{11... | collective-permute-start | bytes 208904 | tf_op jit(solution)/shard_map/ppermute | solution.py:16
  195.5 5.3 %collective-permute-start.40 = (f32[2,1,32,256]{3,1,2,0:T(1,128)S(1)}, f32[2,1,32,256]{3,1,2,0:T(1,128)S(1)}, u32[]{:S(2)}, u32[]{:S(2)}) collective-permute-start(f32[2,1,32,256]{3,1,2,0:T(1,128)S(1)} %get-tuple-element.54), channel_id=1, source_target_pairs={{8,0},{16,8},{24,16},{9,1},{17,9},{25,17},{10,2},{18,10},{26,18},{... | collective-permute-start | bytes 196616 | tf_op jit(solution)/shard_map/ppermute | solution.py:17
  196.8 5.3 %collective-permute-start.41 = (f32[2,1,32,256]{3,1,2,0:T(1,128)S(1)}, f32[2,1,32,256]{3,1,2,0:T(1,128)S(1)}, u32[]{:S(2)}, u32[]{:S(2)}) collective-permute-start(f32[2,1,32,256]{3,1,2,0:T(1,128)S(1)} %get-tuple-element.53), channel_id=1, source_target_pairs={{0,8},{8,16},{16,24},{1,9},{9,17},{17,25},{2,10},{10,18},{18,26},{... | collective-permute-start | bytes 196616 | tf_op jit(solution)/shard_map/ppermute | solution.py:16
  202.2 5.8 %collective-permute-start.42 = (f32[2,34,1,256]{3,1,2,0:T(8,128)S(1)}, f32[2,34,1,256]{3,1,2,0:T(8,128)S(1)}, u32[]{:S(2)}, u32[]{:S(2)}) collective-permute-start(f32[2,34,1,256]{3,1,2,0:T(8,128)S(1)} %get-tuple-element.29), channel_id=1, source_target_pairs={{1,0},{2,1},{3,2},{4,3},{5,4},{6,5},{7,6},{9,8},{10,9},{11,10},{12... | collective-permute-start | bytes 208904 | tf_op jit(solution)/shard_map/ppermute | solution.py:17
  203.5 7.0 %collective-permute-start.43 = (f32[2,34,1,256]{3,1,2,0:T(8,128)S(1)}, f32[2,34,1,256]{3,1,2,0:T(8,128)S(1)}, u32[]{:S(2)}, u32[]{:S(2)}) collective-permute-start(f32[2,34,1,256]{3,1,2,0:T(8,128)S(1)} %get-tuple-element.30), channel_id=1, source_target_pairs={{0,1},{1,2},{2,3},{3,4},{4,5},{5,6},{6,7},{8,9},{9,10},{10,11},{11... | collective-permute-start | bytes 208904 | tf_op jit(solution)/shard_map/ppermute | solution.py:16
  214.0 5.8 %collective-permute-start.44 = (f32[2,1,32,256]{3,1,2,0:T(1,128)S(1)}, f32[2,1,32,256]{3,1,2,0:T(1,128)S(1)}, u32[]{:S(2)}, u32[]{:S(2)}) collective-permute-start(f32[2,1,32,256]{3,1,2,0:T(1,128)S(1)} %get-tuple-element.52), channel_id=1, source_target_pairs={{8,0},{16,8},{24,16},{9,1},{17,9},{25,17},{10,2},{18,10},{26,18},{... | collective-permute-start | bytes 196616 | tf_op jit(solution)/shard_map/ppermute | solution.py:17
  215.3 5.8 %collective-permute-start.45 = (f32[2,1,32,256]{3,1,2,0:T(1,128)S(1)}, f32[2,1,32,256]{3,1,2,0:T(1,128)S(1)}, u32[]{:S(2)}, u32[]{:S(2)}) collective-permute-start(f32[2,1,32,256]{3,1,2,0:T(1,128)S(1)} %get-tuple-element.51), channel_id=1, source_target_pairs={{0,8},{8,16},{16,24},{1,9},{9,17},{17,25},{2,10},{10,18},{18,26},{... | collective-permute-start | bytes 196616 | tf_op jit(solution)/shard_map/ppermute | solution.py:16
  221.1 5.8 %collective-permute-start.46 = (f32[2,34,1,256]{3,1,2,0:T(8,128)S(1)}, f32[2,34,1,256]{3,1,2,0:T(8,128)S(1)}, u32[]{:S(2)}, u32[]{:S(2)}) collective-permute-start(f32[2,34,1,256]{3,1,2,0:T(8,128)S(1)} %get-tuple-element.27), channel_id=1, source_target_pairs={{1,0},{2,1},{3,2},{4,3},{5,4},{6,5},{7,6},{9,8},{10,9},{11,10},{12... | collective-permute-start | bytes 208904 | tf_op jit(solution)/shard_map/ppermute | solution.py:17
  222.4 5.9 %collective-permute-start.47 = (f32[2,34,1,256]{3,1,2,0:T(8,128)S(1)}, f32[2,34,1,256]{3,1,2,0:T(8,128)S(1)}, u32[]{:S(2)}, u32[]{:S(2)}) collective-permute-start(f32[2,34,1,256]{3,1,2,0:T(8,128)S(1)} %get-tuple-element.28), channel_id=1, source_target_pairs={{0,1},{1,2},{2,3},{3,4},{4,5},{5,6},{6,7},{8,9},{9,10},{10,11},{11... | collective-permute-start | bytes 208904 | tf_op jit(solution)/shard_map/ppermute | solution.py:16
  231.6 14.1 %copy-start.4 = (f32[32,32,256]{2,1,0:T(8,128)S(1)}, f32[32,32,256]{2,1,0:T(8,128)}, u32[]{:S(2)}) copy-start(f32[32,32,256]{2,1,0:T(8,128)} %param.7) | copy-start | bytes 3145732
  231.7 6.1 %collective-permute-start.48 = (f32[2,1,32,256]{3,1,2,0:T(1,128)S(1)}, f32[2,1,32,256]{3,1,2,0:T(1,128)S(1)}, u32[]{:S(2)}, u32[]{:S(2)}) collective-permute-start(f32[2,1,32,256]{3,1,2,0:T(1,128)S(1)} %get-tuple-element.50), channel_id=1, source_target_pairs={{8,0},{16,8},{24,16},{9,1},{17,9},{25,17},{10,2},{18,10},{26,18},{... | collective-permute-start | bytes 196616 | tf_op jit(solution)/shard_map/ppermute | solution.py:17
  233.2 5.9 %collective-permute-start.49 = (f32[2,1,32,256]{3,1,2,0:T(1,128)S(1)}, f32[2,1,32,256]{3,1,2,0:T(1,128)S(1)}, u32[]{:S(2)}, u32[]{:S(2)}) collective-permute-start(f32[2,1,32,256]{3,1,2,0:T(1,128)S(1)} %get-tuple-element.49), channel_id=1, source_target_pairs={{0,8},{8,16},{16,24},{1,9},{9,17},{17,25},{2,10},{10,18},{18,26},{... | collective-permute-start | bytes 196616 | tf_op jit(solution)/shard_map/ppermute | solution.py:16
  239.1 7.5 %collective-permute-start.50 = (f32[2,34,1,256]{3,1,2,0:T(8,128)S(1)}, f32[2,34,1,256]{3,1,2,0:T(8,128)S(1)}, u32[]{:S(2)}, u32[]{:S(2)}) collective-permute-start(f32[2,34,1,256]{3,1,2,0:T(8,128)S(1)} %get-tuple-element.25), channel_id=1, source_target_pairs={{1,0},{2,1},{3,2},{4,3},{5,4},{6,5},{7,6},{9,8},{10,9},{11,10},{12... | collective-permute-start | bytes 208904 | tf_op jit(solution)/shard_map/ppermute | solution.py:17
  240.4 6.7 %collective-permute-start.51 = (f32[2,34,1,256]{3,1,2,0:T(8,128)S(1)}, f32[2,34,1,256]{3,1,2,0:T(8,128)S(1)}, u32[]{:S(2)}, u32[]{:S(2)}) collective-permute-start(f32[2,34,1,256]{3,1,2,0:T(8,128)S(1)} %get-tuple-element.26), channel_id=1, source_target_pairs={{0,1},{1,2},{2,3},{3,4},{4,5},{5,6},{6,7},{8,9},{9,10},{10,11},{11... | collective-permute-start | bytes 208904 | tf_op jit(solution)/shard_map/ppermute | solution.py:16
  465.0 30.5 %all-to-all-start.1 = ((f32[8,8,32,256]{3,2,1,0:T(8,128)}), f32[8,8,32,256]{3,2,1,0:T(8,128)S(1)}, u32[]{:S(2)}, u32[]{:S(2)}) async-start(f32[8,8,32,256]{3,2,1,0:T(8,128)} %copy.62), calls=%async_computation.1 | async-start | bytes 4194304 | tf_op jit(solution)/shard_map/all_to_all | solution.py:107
